TPU v7x, 32 devices: a whole 2x2x4 slice. The times are simulated.
32 devices in a mesh: base: 16 (over z, x, core), band: 2 (over y).
Axes of the slice: x: 2, y: 2, z: 4, core: 2. Of those that a mesh axis runs over, the one named last changes fastest.
Arguments:
- coherency: float32 [16, 16, 8, 4096], P('band', None, None, 'base'), may hold values from -1.5 to 1.5
- observed: float32 [16, 8, 4096], P('band', None, 'base'), may hold values from -6 to 6
- jones_deviation: float32 [16, 16, 8, 512], P('band', None, None, 'base'), may hold values from -1.8 to 1.8
- antenna_first: int32 [4096], P('base'), may hold values from 0 to 511, as said below
- antenna_second: int32 [4096], P('base'), may hold values from 0 to 511, as said below
Outputs:
- jones: float32 [16, 16, 8, 512], P('band', None, None, 'base')
- residual: float32 [16, 8, 4096], P('band', None, 'base')
Inputs may be any that keep to these rules, and one draw needn't show every extreme that they name: `antenna_first`: every station is the first station of exactly 8 baselines. On every baseline antenna_second differs from antenna_first.
All inputs are finite; a program needn't handle non-finite values.
Results may differ from a plain program's by a relative error of at most 0.0003.
Values sent between devices are 32-bit elements; how exact they have to be, the bound alone decides.
A program may use at most 128 MiB of HBM per device.

v0:
```python
import jax
import jax.numpy as jnp
from jax import lax
from jax.sharding import PartitionSpec as P

ITERS = 3
step_gain = 1.2
penalty_gain = 0.25


def expand_matrix(packed):
    return [
        [(packed[..., 0, :], packed[..., 1, :]), (packed[..., 2, :], packed[..., 3, :])],
        [(packed[..., 4, :], packed[..., 5, :]), (packed[..., 6, :], packed[..., 7, :])],
    ]


def pack_matrix(matrix):
    return jnp.stack(
        [
            matrix[0][0][0],
            matrix[0][0][1],
            matrix[0][1][0],
            matrix[0][1][1],
            matrix[1][0][0],
            matrix[1][0][1],
            matrix[1][1][0],
            matrix[1][1][1],
        ],
        axis=-2,
    )


def complex_mul(first_term, second_term):
    return (
        first_term[0] * second_term[0] - first_term[1] * second_term[1],
        first_term[0] * second_term[1] + first_term[1] * second_term[0],
    )


def complex_add(first_term, second_term):
    return (first_term[0] + second_term[0], first_term[1] + second_term[1])


def element_of(matrix, i, j, adjoint):
    if adjoint:
        return (matrix[j][i][0], -matrix[j][i][1])
    return matrix[i][j]


def matrix_product(first_factor, second_factor, adjoint_first=False, adjoint_second=False):
    result_rows = []
    for i in range(2):
        row_items = []
        for j in range(2):
            row_items.append(
                complex_add(
                    complex_mul(
                        element_of(first_factor, i, 0, adjoint_first),
                        element_of(second_factor, 0, j, adjoint_second),
                    ),
                    complex_mul(
                        element_of(first_factor, i, 1, adjoint_first),
                        element_of(second_factor, 1, j, adjoint_second),
                    ),
                )
            )
        result_rows.append(row_items)
    return result_rows


def fit_basis(band_count):
    positions = (2.0 * jnp.arange(band_count, dtype=jnp.float32) + 1.0) / band_count - 1.0
    columns = []
    for power in range(4):
        vector = positions**power
        for earlier in columns:
            vector = vector - jnp.sum(earlier * vector) * earlier
        vector = vector / jnp.sqrt(jnp.sum(vector * vector))
        columns.append(vector)
    return jnp.stack(columns, axis=1)


def local_gradients(
    leading_rows, trailing_rows, coherency, observed, antenna_first, antenna_second, station_number
):
    leading_jones = expand_matrix(leading_rows)
    trailing_jones = expand_matrix(trailing_rows)
    sky = expand_matrix(coherency)
    model = pack_matrix(
        matrix_product(leading_jones, matrix_product(sky, trailing_jones, adjoint_second=True))
    )
    residual = observed - jnp.sum(model, axis=1)
    resid_parts = expand_matrix(residual[:, None])
    gradient_leading = pack_matrix(
        matrix_product(resid_parts, matrix_product(trailing_jones, sky, adjoint_second=True))
    )
    gradient_trailing = pack_matrix(
        matrix_product(resid_parts, matrix_product(leading_jones, sky), adjoint_first=True)
    )
    shape_out = (coherency.shape[0], coherency.shape[1], 8, station_number)
    gradient_list = (
        jnp.zeros(shape_out, jnp.float32)
        .at[:, :, :, antenna_first]
        .add(gradient_leading)
        .at[:, :, :, antenna_second]
        .add(gradient_trailing)
    )
    return (gradient_list, residual)


def per_device(coherency, observed, jones_deviation, antenna_first, antenna_second):
    highest = lax.Precision.HIGHEST
    base_count = lax.axis_size("base")
    band_count = lax.axis_size("band")
    sub_dev = coherency.shape[0]
    base_dev = coherency.shape[-1]
    own_stations = jones_deviation.shape[-1]
    station_number = own_stations * base_count
    baseline_count = base_dev * base_count
    step_size = step_gain * station_number / baseline_count
    penalty = penalty_gain * baseline_count / station_number
    poly_basis = fit_basis(sub_dev * band_count)
    local_basis = lax.dynamic_slice_in_dim(poly_basis, lax.axis_index("band") * sub_dev, sub_dev, 0)
    identity = jnp.array([1.0, 0.0, 0.0, 0.0, 0.0, 0.0, 1.0, 0.0], dtype=jnp.float32)[:, None]
    jones_current = identity + jones_deviation
    jones_current = lax.all_gather(jones_current, "base", axis=3, tiled=True)
    consensus = jones_current
    dual_var = jnp.zeros_like(jones_current)
    residual = None
    for iteration in range(ITERS):
        leading_rows = jnp.take(jones_current, antenna_first, axis=3)
        trailing_rows = jnp.take(jones_current, antenna_second, axis=3)
        local_terms, residual = local_gradients(
            leading_rows,
            trailing_rows,
            coherency,
            observed,
            antenna_first,
            antenna_second,
            station_number,
        )
        station_gradients = lax.psum(local_terms, "base")
        jones_current = jones_current + step_size * (
            station_gradients - dual_var - penalty * (jones_current - consensus)
        )
        if iteration + 1 < ITERS:
            target = jones_current + dual_var / penalty
            partial_fit = jnp.einsum("fm,fkcs->mkcs", local_basis, target, precision=highest)
            coefficients = lax.psum(partial_fit, "band")
            consensus = jnp.einsum("fm,mkcs->fkcs", local_basis, coefficients, precision=highest)
            dual_var = dual_var + penalty * (jones_current - consensus)
    jones_current = lax.dynamic_slice_in_dim(
        jones_current, lax.axis_index("base") * own_stations, own_stations, 3
    )
    return (jones_current, residual)


def solution(mesh):
    return jax.shard_map(
        per_device,
        mesh=mesh,
        in_specs=(
            P("band", None, None, "base"),
            P("band", None, "base"),
            P("band", None, None, "base"),
            P("base"),
            P("base"),
        ),
        out_specs=(P("band", None, None, "base"), P("band", None, "base")),
        check_vma=False,
    )
```

profile of v0, /device:TPU:0, one launch (start us, length us, event | category | flops | bytes accessed | tf_op | source)
XLA Modules:
  0.0 1139.3 jit_solution(16276159739745969013)
XLA Ops:
  19.4 120.1 %all-gather.2.cloned.1.call-done = f32[8,16,8,512]{1,2,0,3:T(8,128)} async-done(((f32[8,16,8,32]{1,2,0,3:T(8,128)}), f32[8,16,8,512]{1,2,0,3:T(8,128)}) %all-gather.2.cloned.1.call-update) | async-done | bytes 2097168 | tf_op jit(solution)/shard_map/all_gather | solution.py:127
  139.5 11.4 copy.497
  150.9 10.6 gather_fusion
  168.6 10.6 gather_fusion.1
  254.8 39.8 %scatter_fusion = f32[8,16,8,512]{1,2,3,0:T(8,128)} fusion(f32[8,16,8,512]{1,2,3,0:T(8,128)} %broadcast.414.clone, s32[256]{0:T(256)S(1)} %copy-done.42, f32[256,8,16,8]{2,3,1,0:T(8,128)} %copy.527), kind=kCustom, calls=%fused_computation.6 | custom fusion | flops 262144 | bytes 3146752 | tf_op jit(solution)/shard_map/scatter-add | solution.py:105
  294.7 39.9 %scatter_fusion.1 = f32[8,16,8,512]{1,2,3,0:T(8,128)} fusion(f32[8,16,8,512]{1,2,3,0:T(8,128)} %scatter_fusion, s32[256]{0:T(256)S(1)} %copy-done.38, f32[256,8,16,8]{2,3,1,0:T(8,128)} %copy.536), kind=kCustom, calls=%fused_computation.7 | custom fusion | flops 262144 | bytes 3146752 | tf_op jit(solution)/shard_map/scatter-add | solution.py:107
  334.6 9.7 copy.537
  350.6 12.2 %copy.540 = f32[8,16,8,512]{3,0,2,1:T(8,128)} copy(f32[8,16,8,512]{1,2,0,3:T(8,128)} %all-gather.2.cloned.1.call-done) | data formatting | bytes 4194304 | tf_op jit(solution)/shard_map/all_gather | solution.py:127
  362.8 78.2 %all-reduce.6.cloned.1.call-done = f32[8,16,8,512]{3,0,2,1:T(8,128)} async-done(((f32[8,16,8,512]{3,0,2,1:T(8,128)}), f32[8,16,8,512]{3,0,2,1:T(8,128)}) %all-reduce.6.cloned.1.call-update) | async-done | bytes 2097168 | tf_op jit(solution)/shard_map/psum | solution.py:143
  443.8 7.8 copy.541
  451.6 10.8 gather_fusion.2
  462.4 10.8 gather_fusion.3
  586.2 39.8 %scatter_fusion.2 = f32[8,16,8,512]{1,2,3,0:T(8,128)} fusion(f32[8,16,8,512]{1,2,3,0:T(8,128)} %broadcast.414.clone.1, s32[256]{0:T(256)S(1)} %copy-done.43, f32[256,8,16,8]{2,3,1,0:T(8,128)} %copy.563), kind=kCustom, calls=%fused_computation.8 | custom fusion | flops 262144 | bytes 3146752 | tf_op jit(solution)/shard_map/scatter-add | solution.py:105
  626.0 39.8 %scatter_fusion.3 = f32[8,16,8,512]{1,2,3,0:T(8,128)} fusion(f32[8,16,8,512]{1,2,3,0:T(8,128)} %scatter_fusion.2, s32[256]{0:T(256)S(1)} %copy-done.39, f32[256,8,16,8]{2,3,1,0:T(8,128)} %copy.572), kind=kCustom, calls=%fused_computation.9 | custom fusion | flops 262144 | bytes 3146752 | tf_op jit(solution)/shard_map/scatter-add | solution.py:107
  665.8 9.7 copy.573
  686.7 86.7 %all-reduce.8.cloned.1.call-done = f32[8,16,8,512]{3,0,2,1:T(8,128)} async-done(((f32[8,16,8,512]{3,0,2,1:T(8,128)}), f32[8,16,8,512]{3,0,2,1:T(8,128)}) %all-reduce.8.cloned.1.call-update) | async-done | bytes 2097168 | tf_op jit(solution)/shard_map/psum | solution.py:143
  773.5 41.6 %all-reduce.10.cloned.1.call-done = f32[4,16,8,512]{3,0,2,1:T(4,128)} async-done(((f32[4,16,8,512]{3,0,2,1:T(4,128)}), f32[4,16,8,512]{3,0,2,1:T(4,128)}) %all-reduce.10.cloned.1.call-update) | async-done | bytes 1048592 | tf_op jit(solution)/shard_map/psum | solution.py:150
  828.8 10.8 gather_fusion.4
  839.6 10.8 gather_fusion.5
  912.8 8.4 copy.596
  940.7 39.8 %scatter_fusion.4 = f32[8,16,8,512]{1,2,3,0:T(8,128)} fusion(f32[8,16,8,512]{1,2,3,0:T(8,128)} %broadcast.414, s32[256]{0:T(256)S(1)} %copy-done.44, f32[256,8,16,8]{2,3,1,0:T(8,128)} %copy.596), kind=kCustom, calls=%fused_computation.10 | custom fusion | flops 262144 | bytes 3146752 | tf_op jit(solution)/shard_map/scatter-add | solution.py:105
  980.5 39.8 %scatter_fusion.5 = f32[8,16,8,512]{1,2,3,0:T(8,128)} fusion(f32[8,16,8,512]{1,2,3,0:T(8,128)} %scatter_fusion.4, s32[256]{0:T(256)S(1)} %copy-done.40, f32[256,8,16,8]{2,3,1,0:T(8,128)} %copy.605), kind=kCustom, calls=%fused_computation.11 | custom fusion | flops 262144 | bytes 3146752 | tf_op jit(solution)/shard_map/scatter-add | solution.py:107
  1020.3 10.1 copy.606
  1036.3 92.8 %all-reduce.12.cloned.1.call-done = f32[8,16,8,512]{3,0,2,1:T(8,128)} async-done(((f32[8,16,8,512]{3,0,2,1:T(8,128)}), f32[8,16,8,512]{3,0,2,1:T(8,128)}) %all-reduce.12.cloned.1.call-update) | async-done | bytes 2097168 | tf_op jit(solution)/shard_map/psum | solution.py:143
  (313 shorter events, 327.9 us)
Async XLA Ops:
  7.2 132.3 %all-gather.2.cloned.1.call-start = ((), (), s32[]{:S(2)}) async-start(), calls=%async_computation | async-start | bytes 17825792 | tf_op jit(solution)/shard_map/all_gather | solution.py:127
  10.2 430.8 %all-reduce.6.cloned.1.call-start = ((), (), s32[]{:S(2)}) async-start(), calls=%async_computation.1 | async-start | bytes 4194304 | tf_op jit(solution)/shard_map/psum | solution.py:143
  11.5 187.3 %copy-start.13 = (f32[8,8,256]{1,0,2:T(8,128)}, f32[8,8,256]{1,0,2:T(8,128)S(1)}, u32[]{:S(2)}) copy-start(f32[8,8,256]{1,0,2:T(8,128)S(1)} %copy.510) | copy-start | bytes 196612
  12.3 138.6 %copy-start.45 = (s32[1024]{0:T(1024)}, s32[1024]{0:T(1024)S(1)}, u32[]{:S(2)}) copy-start(s32[1024]{0:T(1024)S(1)} %pad_clamp_fusion.1) | copy-start | bytes 12292
  12.9 155.8 %copy-start.46 = (s32[1024]{0:T(1024)}, s32[1024]{0:T(1024)S(1)}, u32[]{:S(2)}) copy-start(s32[1024]{0:T(1024)S(1)} %pad_clamp_fusion) | copy-start | bytes 12292
  13.6 173.3 %copy-start.50 = (pred[256]{0:T(512)(128)(4,1)}, pred[256]{0:T(512)(128)(4,1)S(1)}, u32[]{:S(2)}) copy-start(pred[256]{0:T(512)(128)(4,1)S(1)} %get-tuple-element.206) | copy-start | bytes 772
  13.6 174.7 %copy-start.47 = (pred[256]{0:T(512)(128)(4,1)}, pred[256]{0:T(512)(128)(4,1)S(1)}, u32[]{:S(2)}) copy-start(pred[256]{0:T(512)(128)(4,1)S(1)} %get-tuple-element.205) | copy-start | bytes 772
  19.3 198.3 %copy-start.5 = (f32[8,16,1,256]{3,2,1,0:T(1,128)}, f32[8,16,1,256]{3,2,1,0:T(1,128)S(1)}, u32[]{:S(2)}) copy-start(f32[8,16,1,256]{3,2,1,0:T(1,128)S(1)} %get-tuple-element.140) | copy-start | bytes 393220
  19.3 198.3 %copy-start.7 = (f32[8,16,1,256]{3,2,1,0:T(1,128)}, f32[8,16,1,256]{3,2,1,0:T(1,128)S(1)}, u32[]{:S(2)}) copy-start(f32[8,16,1,256]{3,2,1,0:T(1,128)S(1)} %get-tuple-element.142) | copy-start | bytes 393220
  19.4 198.3 %copy-start.9 = (f32[8,16,1,256]{3,2,1,0:T(1,128)}, f32[8,16,1,256]{3,2,1,0:T(1,128)S(1)}, u32[]{:S(2)}) copy-start(f32[8,16,1,256]{3,2,1,0:T(1,128)S(1)} %get-tuple-element.145) | copy-start | bytes 393220
  19.4 198.3 %copy-start.11 = (f32[8,16,1,256]{3,2,1,0:T(1,128)}, f32[8,16,1,256]{3,2,1,0:T(1,128)S(1)}, u32[]{:S(2)}) copy-start(f32[8,16,1,256]{3,2,1,0:T(1,128)S(1)} %get-tuple-element.146) | copy-start | bytes 393220
  19.4 199.8 %copy-start.3 = (f32[8,16,1,256]{3,2,1,0:T(1,128)}, f32[8,16,1,256]{3,2,1,0:T(1,128)S(1)}, u32[]{:S(2)}) copy-start(f32[8,16,1,256]{3,2,1,0:T(1,128)S(1)} %get-tuple-element.147) | copy-start | bytes 393220
  247.8 46.9 %copy-start.38 = (s32[256]{0:T(256)S(1)}, s32[256]{0:T(256)}, u32[]{:S(2)}) copy-start(s32[256]{0:T(256)} %copy-done.37) | copy-start | bytes 3076
  344.3 429.2 %all-reduce.8.cloned.1.call-start = ((), (), s32[]{:S(2)}) async-start(), calls=%async_computation.2 | async-start | bytes 4194304 | tf_op jit(solution)/shard_map/psum | solution.py:143
  443.8 240.0 %copy-start.2 = (f32[8,16,8,512]{3,0,2,1:T(8,128)}, f32[8,16,8,512]{3,0,2,1:T(8,128)S(1)}, u32[]{:S(2)}) copy-start(f32[8,16,8,512]{3,0,2,1:T(8,128)S(1)} %multiply_add_fusion) | copy-start | bytes 6291460
  451.6 28.7 %copy-start.51 = (pred[256]{0:T(512)(128)(4,1)S(1)}, pred[256]{0:T(512)(128)(4,1)}, u32[]{:S(2)}) copy-start(pred[256]{0:T(512)(128)(4,1)} %copy-done.50) | copy-start | bytes 772
  473.2 16.0 %copy-start.48 = (pred[256]{0:T(512)(128)(4,1)S(1)}, pred[256]{0:T(512)(128)(4,1)}, u32[]{:S(2)}) copy-start(pred[256]{0:T(512)(128)(4,1)} %copy-done.47) | copy-start | bytes 772
  579.1 46.9 %copy-start.39 = (s32[256]{0:T(256)S(1)}, s32[256]{0:T(256)}, u32[]{:S(2)}) copy-start(s32[256]{0:T(256)} %copy-done.37) | copy-start | bytes 3076
  675.5 139.5 %all-reduce.10.cloned.1.call-start = ((), (), s32[]{:S(2)}) async-start(), calls=%async_computation.3 | async-start | bytes 2097152 | tf_op jit(solution)/shard_map/psum | solution.py:150
  683.8 145.0 %copy-start.35 = (f32[16,4]{0,1:T(4,128)}, f32[16,4]{0,1:T(4,128)S(1)}, u32[]{:S(2)}) copy-start(f32[16,4]{0,1:T(4,128)S(1)} %pad_maximum_fusion) | copy-start | bytes 772
  686.7 344.7 %all-reduce.14.cloned.1.call-start = ((), (), s32[]{:S(2)}) async-start(), calls=%async_computation.5 | async-start | bytes 2097152 | tf_op jit(solution)/shard_map/psum | solution.py:150
  828.8 27.8 %copy-start.52 = (pred[256]{0:T(512)(128)(4,1)S(1)}, pred[256]{0:T(512)(128)(4,1)}, u32[]{:S(2)}) copy-start(pred[256]{0:T(512)(128)(4,1)} %copy-done.50) | copy-start | bytes 772
  900.9 228.2 %all-reduce.12.cloned.1.call-start = ((), (), s32[]{:S(2)}) async-start(), calls=%async_computation.4 | async-start | bytes 4194304 | tf_op jit(solution)/shard_map/psum | solution.py:143
  933.6 46.9 %copy-start.40 = (s32[256]{0:T(256)S(1)}, s32[256]{0:T(256)}, u32[]{:S(2)}) copy-start(s32[256]{0:T(256)} %copy-done.37) | copy-start | bytes 3076
  (36 other events, 244.2 us)
Sparse Core Ops, SparseCore 0:
  10.3 129.1 all-gather.1
  344.4 96.5 all-reduce.5
  675.6 97.8 all-reduce.7
  775.6 39.3 all-reduce.9
  901.0 40.0 all-reduce.13
  1030.6 98.4 all-reduce.11
where the time goes:
time: 1150 us; the launch traced here: 1140 us
  waiting for transfers between devices  419 us (36%)
  local copies, waits for them, and re-layouts  357 us (31%)
  other arithmetic  324 us (28%)
  between operations  19.6 us (2%)
  matrix products  18.7 us (2%)
    psum x3, waiting for transfers between devices, per_device(): station_gradients = lax.psum(local_terms, 'base')  258 us
    scatter-add x6, other arithmetic, local_gradients(): gradient_list = jnp.zeros(shape_out, jnp.float32).at[:, :, :, antenna_fir...  239 us
    all_gather x1, waiting for transfers between devices, per_device(): jones_current = lax.all_gather(jones_current, 'base', axis=3, tiled=True)  120 us
    another operation x12, local copies, waits for them, and re-layouts, pack_matrix(): jnp.stack([matrix[0][0][0], matrix[0][0][1], matrix[0][1][0], matrix[0][1...  61.1 us
    gather x6, local copies, waits for them, and re-layouts, per_device(): trailing_rows = jnp.take(jones_current, antenna_second, axis=3)  53.9 us
    gather x6, local copies, waits for them, and re-layouts, per_device(): leading_rows = jnp.take(jones_current, antenna_first, axis=3)  52.7 us
    psum x2, waiting for transfers between devices, per_device(): coefficients = lax.psum(partial_fit, 'band')  41.6 us
    scatter-add x3, local copies, waits for them, and re-layouts, local_gradients(): gradient_list = jnp.zeros(shape_out, jnp.float32).at[:, :, :, antenna_fir...  29.5 us
  transfers between devices with their start and end apart: 6, of which 5 were waited for; matrix products, arithmetic and copies ran while one was open for 15% of the time, Pallas kernels for 0%

commit v1 on v0

--- a/solution.py
+++ b/solution.py
@@ -140,7 +140,11 @@
             antenna_second,
             station_number,
         )
-        station_gradients = lax.psum(local_terms, "base")
+        station_gradients = local_terms
+        for hop in (1, 2, 4, 8):
+            station_gradients = station_gradients + lax.ppermute(
+                station_gradients, "base", [(dev, dev ^ hop) for dev in range(16)]
+            )
         jones_current = jones_current + step_size * (
             station_gradients - dual_var - penalty * (jones_current - consensus)
         )

time: 1150 us -> 1370 us (1.19)
  waiting for transfers between devices: 419 us -> 653 us
  local copies, waits for them, and re-layouts: 357 us -> 340 us
    ppermute x0 -> x12, waiting for transfers between devices: none -> 447 us  [per_device(): lax.ppermute(station_gradients, 'base', [(dev, dev ^ hop) for dev in rang...]
    psum x3 -> x0, waiting for transfers between devices: 258 us -> none  [per_device(): station_gradients = lax.psum(local_terms, 'base')]
    psum x2, waiting for transfers between devices: 41.6 us -> 79.1 us  [per_device(): coefficients = lax.psum(partial_fit, 'band')]
  transfers between devices with their start and end apart: 6 -> 15, of which waited for: 5 -> 15; matrix products, arithmetic and copies ran while one was open for 15% -> 3% of each run, Pallas kernels for 0% -> 0%
where the time goes in v1:
time: 1370 us; the launch traced here: 1360 us
  waiting for transfers between devices  653 us (48%)
  local copies, waits for them, and re-layouts  340 us (25%)
  other arithmetic  330 us (24%)
  between operations  19.8 us (1%)
    ppermute x12, waiting for transfers between devices, per_device(): lax.ppermute(station_gradients, 'base', [(dev, dev ^ hop) for dev in rang...  447 us
    scatter-add x6, other arithmetic, local_gradients(): gradient_list = jnp.zeros(shape_out, jnp.float32).at[:, :, :, antenna_fir...  239 us
    all_gather x1, waiting for transfers between devices, per_device(): jones_current = lax.all_gather(jones_current, 'base', axis=3, tiled=True)  127 us
    psum x2, waiting for transfers between devices, per_device(): coefficients = lax.psum(partial_fit, 'band')  79.1 us
    another operation x12, local copies, waits for them, and re-layouts, pack_matrix(): jnp.stack([matrix[0][0][0], matrix[0][0][1], matrix[0][1][0], matrix[0][1...  58.3 us
    gather x6, local copies, waits for them, and re-layouts, per_device(): trailing_rows = jnp.take(jones_current, antenna_second, axis=3)  53.3 us
    gather x6, local copies, waits for them, and re-layouts, per_device(): leading_rows = jnp.take(jones_current, antenna_first, axis=3)  52.9 us
  transfers between devices with their start and end apart: 15, of which 15 were waited for; matrix products, arithmetic and copies ran while one was open for 3% of the time, Pallas kernels for 0%

profile of v1, /device:TPU:0, one launch (start us, length us, event | category | flops | bytes accessed | tf_op | source)
XLA Modules:
  0.0 1362.7 jit_solution(17642716645432341245)
XLA Ops:
  12.5 127.0 %all-gather.2.cloned.1.call-done = f32[8,16,8,512]{1,2,0,3:T(8,128)} async-done(((f32[8,16,8,32]{1,2,0,3:T(8,128)}), f32[8,16,8,512]{1,2,0,3:T(8,128)}) %all-gather.2.cloned.1.call-update) | async-done | bytes 2097168 | tf_op jit(solution)/shard_map/all_gather | solution.py:127
  139.5 11.4 copy.512
  254.3 40.0 %scatter_fusion = f32[8,16,8,512]{1,2,3,0:T(8,128)} fusion(f32[8,16,8,512]{1,2,3,0:T(8,128)} %broadcast.414.clone, s32[256]{0:T(256)S(1)} %copy-done.110, f32[256,8,16,8]{2,3,1,0:T(8,128)} %copy.542), kind=kCustom, calls=%fused_computation.6 | custom fusion | flops 262144 | bytes 3146752 | tf_op jit(solution)/shard_map/scatter-add | solution.py:105
  294.3 40.2 %scatter_fusion.1 = f32[8,16,8,512]{1,2,3,0:T(8,128)} fusion(f32[8,16,8,512]{1,2,3,0:T(8,128)} %scatter_fusion, s32[256]{0:T(256)S(1)} %copy-done.106, f32[256,8,16,8]{2,3,1,0:T(8,128)} %copy.551), kind=kCustom, calls=%fused_computation.7 | custom fusion | flops 262144 | bytes 3146752 | tf_op jit(solution)/shard_map/scatter-add | solution.py:107
  348.3 47.3 %collective-permute-done.1 = f32[8,16,8,512]{3,0,2,1:T(8,128)S(1)} collective-permute-done((f32[8,16,8,512]{3,0,2,1:T(8,128)S(1)}, f32[8,16,8,512]{3,0,2,1:T(8,128)S(1)}, u32[]{:S(2)}, u32[]{:S(2)}) %collective-permute-start.1) | collective-permute-done | bytes 2097184 | tf_op jit(solution)/shard_map/ppermute | solution.py:145
  396.2 46.8 %collective-permute-done.2 = f32[8,16,8,512]{3,0,2,1:T(8,128)S(1)} collective-permute-done((f32[8,16,8,512]{3,0,2,1:T(8,128)S(1)}, f32[8,16,8,512]{3,0,2,1:T(8,128)S(1)}, u32[]{:S(2)}, u32[]{:S(2)}) %collective-permute-start.2) | collective-permute-done | bytes 2097184 | tf_op jit(solution)/shard_map/ppermute | solution.py:145
  445.3 12.2 copy.556
  457.5 77.9 %collective-permute-done.3 = f32[8,16,8,512]{3,0,2,1:T(8,128)} collective-permute-done((f32[8,16,8,512]{3,0,2,1:T(8,128)S(1)}, f32[8,16,8,512]{3,0,2,1:T(8,128)}, u32[]{:S(2)}, u32[]{:S(2)}) %collective-permute-start.3) | collective-permute-done | bytes 2097184 | tf_op jit(solution)/shard_map/ppermute | solution.py:145
  546.9 10.8 gather_fusion.2
  557.7 10.9 gather_fusion.3
  673.8 39.8 %scatter_fusion.2 = f32[8,16,8,512]{1,2,3,0:T(8,128)} fusion(f32[8,16,8,512]{1,2,3,0:T(8,128)} %broadcast.414.clone.1, s32[256]{0:T(256)S(1)} %copy-done.111, f32[256,8,16,8]{2,3,1,0:T(8,128)} %copy.579), kind=kCustom, calls=%fused_computation.8 | custom fusion | flops 262144 | bytes 3146752 | tf_op jit(solution)/shard_map/scatter-add | solution.py:105
  713.6 39.8 %scatter_fusion.3 = f32[8,16,8,512]{1,2,3,0:T(8,128)} fusion(f32[8,16,8,512]{1,2,3,0:T(8,128)} %scatter_fusion.2, s32[256]{0:T(256)S(1)} %copy-done.107, f32[256,8,16,8]{2,3,1,0:T(8,128)} %copy.588), kind=kCustom, calls=%fused_computation.9 | custom fusion | flops 262144 | bytes 3146752 | tf_op jit(solution)/shard_map/scatter-add | solution.py:107
  770.9 46.4 %collective-permute-done.5 = f32[8,16,8,512]{3,0,2,1:T(8,128)S(1)} collective-permute-done((f32[8,16,8,512]{3,0,2,1:T(8,128)S(1)}, f32[8,16,8,512]{3,0,2,1:T(8,128)S(1)}, u32[]{:S(2)}, u32[]{:S(2)}) %collective-permute-start.5) | collective-permute-done | bytes 2097184 | tf_op jit(solution)/shard_map/ppermute | solution.py:145
  828.6 37.6 %collective-permute-done.6 = f32[8,16,8,512]{3,0,2,1:T(8,128)} collective-permute-done((f32[8,16,8,512]{3,0,2,1:T(8,128)}, f32[8,16,8,512]{3,0,2,1:T(8,128)}, u32[]{:S(2)}, u32[]{:S(2)}) %collective-permute-start.6) | collective-permute-done | bytes 2097184 | tf_op jit(solution)/shard_map/ppermute | solution.py:145
  878.5 39.8 %all-reduce.3.cloned.1.call-done = f32[4,16,8,512]{3,0,2,1:T(4,128)} async-done(((f32[4,16,8,512]{3,0,2,1:T(4,128)}), f32[4,16,8,512]{3,0,2,1:T(4,128)}) %all-reduce.3.cloned.1.call-update) | async-done | bytes 1048592 | tf_op jit(solution)/shard_map/psum | solution.py:154
  921.9 40.5 %collective-permute-done.7 = f32[8,16,8,512]{3,0,2,1:T(8,128)} collective-permute-done((f32[8,16,8,512]{3,0,2,1:T(8,128)}, f32[8,16,8,512]{3,0,2,1:T(8,128)}, u32[]{:S(2)}, u32[]{:S(2)}) %collective-permute-start.7) | collective-permute-done | bytes 2097184 | tf_op jit(solution)/shard_map/ppermute | solution.py:145
  976.3 10.9 gather_fusion.4
  987.1 10.8 gather_fusion.5
  1071.0 39.8 %scatter_fusion.4 = f32[8,16,8,512]{1,2,3,0:T(8,128)} fusion(f32[8,16,8,512]{1,2,3,0:T(8,128)} %broadcast.414, s32[256]{0:T(256)S(1)} %copy-done.112, f32[256,8,16,8]{2,3,1,0:T(8,128)} %copy.613), kind=kCustom, calls=%fused_computation.10 | custom fusion | flops 262144 | bytes 3146752 | tf_op jit(solution)/shard_map/scatter-add | solution.py:105
  1110.7 39.8 %scatter_fusion.5 = f32[8,16,8,512]{1,2,3,0:T(8,128)} fusion(f32[8,16,8,512]{1,2,3,0:T(8,128)} %scatter_fusion.4, s32[256]{0:T(256)S(1)} %copy-done.108, f32[256,8,16,8]{2,3,1,0:T(8,128)} %copy.622), kind=kCustom, calls=%fused_computation.11 | custom fusion | flops 262144 | bytes 3146752 | tf_op jit(solution)/shard_map/scatter-add | solution.py:107
  1165.4 46.2 %collective-permute-done.9 = f32[8,16,8,512]{3,0,2,1:T(8,128)S(1)} collective-permute-done((f32[8,16,8,512]{3,0,2,1:T(8,128)S(1)}, f32[8,16,8,512]{3,0,2,1:T(8,128)S(1)}, u32[]{:S(2)}, u32[]{:S(2)}) %collective-permute-start.9) | collective-permute-done | bytes 2097184 | tf_op jit(solution)/shard_map/ppermute | solution.py:145
  1212.2 46.8 %collective-permute-done.10 = f32[8,16,8,512]{3,0,2,1:T(8,128)S(1)} collective-permute-done((f32[8,16,8,512]{3,0,2,1:T(8,128)S(1)}, f32[8,16,8,512]{3,0,2,1:T(8,128)S(1)}, u32[]{:S(2)}, u32[]{:S(2)}) %collective-permute-start.10) | collective-permute-done | bytes 2097184 | tf_op jit(solution)/shard_map/ppermute | solution.py:145
  1265.3 39.3 %all-reduce.5.cloned.1.call-done = f32[4,16,8,512]{3,0,2,1:T(4,128)} async-done(((f32[4,16,8,512]{3,0,2,1:T(4,128)}), f32[4,16,8,512]{3,0,2,1:T(4,128)}) %all-reduce.5.cloned.1.call-update) | async-done | bytes 1048592 | tf_op jit(solution)/shard_map/psum | solution.py:154
  1308.1 44.8 %collective-permute-done.11 = f32[8,16,8,512]{3,0,2,1:T(8,128)} collective-permute-done((f32[8,16,8,512]{3,0,2,1:T(8,128)}, f32[8,16,8,512]{3,0,2,1:T(8,128)}, u32[]{:S(2)}, u32[]{:S(2)}) %collective-permute-start.11) | collective-permute-done | bytes 2097184 | tf_op jit(solution)/shard_map/ppermute | solution.py:145
  (476 shorter events, 396.3 us)
Async XLA Ops:
  7.2 132.4 %all-gather.2.cloned.1.call-start = ((), (), s32[]{:S(2)}) async-start(), calls=%async_computation | async-start | bytes 17825792 | tf_op jit(solution)/shard_map/all_gather | solution.py:127
  10.2 908.0 %all-reduce.3.cloned.1.call-start = ((), (), s32[]{:S(2)}) async-start(), calls=%async_computation.1 | async-start | bytes 2097152 | tf_op jit(solution)/shard_map/psum | solution.py:154
  10.7 186.9 %copy-start.22 = (f32[8,8,256]{1,0,2:T(8,128)}, f32[8,8,256]{1,0,2:T(8,128)S(1)}, u32[]{:S(2)}) copy-start(f32[8,8,256]{1,0,2:T(8,128)S(1)} %copy.525) | copy-start | bytes 196612
  11.3 157.4 %copy-start.114 = (s32[1024]{0:T(1024)}, s32[1024]{0:T(1024)S(1)}, u32[]{:S(2)}) copy-start(s32[1024]{0:T(1024)S(1)} %pad_clamp_fusion) | copy-start | bytes 12292
  11.4 175.3 %copy-start.118 = (pred[256]{0:T(512)(128)(4,1)}, pred[256]{0:T(512)(128)(4,1)S(1)}, u32[]{:S(2)}) copy-start(pred[256]{0:T(512)(128)(4,1)S(1)} %get-tuple-element.205) | copy-start | bytes 772
  11.4 176.8 %copy-start.115 = (pred[256]{0:T(512)(128)(4,1)}, pred[256]{0:T(512)(128)(4,1)S(1)}, u32[]{:S(2)}) copy-start(pred[256]{0:T(512)(128)(4,1)S(1)} %get-tuple-element.204) | copy-start | bytes 772
  12.5 204.8 %copy-start.6 = (f32[8,16,1,256]{3,2,1,0:T(1,128)}, f32[8,16,1,256]{3,2,1,0:T(1,128)S(1)}, u32[]{:S(2)}) copy-start(f32[8,16,1,256]{3,2,1,0:T(1,128)S(1)} %get-tuple-element.140) | copy-start | bytes 393220
  12.5 204.8 %copy-start.10 = (f32[8,16,1,256]{3,2,1,0:T(1,128)}, f32[8,16,1,256]{3,2,1,0:T(1,128)S(1)}, u32[]{:S(2)}) copy-start(f32[8,16,1,256]{3,2,1,0:T(1,128)S(1)} %get-tuple-element.142) | copy-start | bytes 393220
  12.5 204.8 %copy-start.14 = (f32[8,16,1,256]{3,2,1,0:T(1,128)}, f32[8,16,1,256]{3,2,1,0:T(1,128)S(1)}, u32[]{:S(2)}) copy-start(f32[8,16,1,256]{3,2,1,0:T(1,128)S(1)} %get-tuple-element.145) | copy-start | bytes 393220
  12.5 204.8 %copy-start.17 = (f32[8,16,1,256]{3,2,1,0:T(1,128)}, f32[8,16,1,256]{3,2,1,0:T(1,128)S(1)}, u32[]{:S(2)}) copy-start(f32[8,16,1,256]{3,2,1,0:T(1,128)S(1)} %get-tuple-element.146) | copy-start | bytes 393220
  12.5 206.4 %copy-start.1 = (f32[8,16,1,256]{3,2,1,0:T(1,128)}, f32[8,16,1,256]{3,2,1,0:T(1,128)S(1)}, u32[]{:S(2)}) copy-start(f32[8,16,1,256]{3,2,1,0:T(1,128)S(1)} %get-tuple-element.147) | copy-start | bytes 393220
  343.1 4.2 collective-permute-start
  347.8 47.7 %collective-permute-start.1 = (f32[8,16,8,512]{3,0,2,1:T(8,128)S(1)}, f32[8,16,8,512]{3,0,2,1:T(8,128)S(1)}, u32[]{:S(2)}, u32[]{:S(2)}) collective-permute-start(f32[8,16,8,512]{3,0,2,1:T(8,128)S(1)} %add.1832), channel_id=1, source_target_pairs={{0,4},{2,6},{4,0},{6,2},{8,12},{10,14},{12,8},{14,10},{16,20},{18,... | collective-permute-start | bytes 6291464 | tf_op jit(solution)/shard_map/ppermute | solution.py:145
  396.1 46.9 %collective-permute-start.2 = (f32[8,16,8,512]{3,0,2,1:T(8,128)S(1)}, f32[8,16,8,512]{3,0,2,1:T(8,128)S(1)}, u32[]{:S(2)}, u32[]{:S(2)}) collective-permute-start(f32[8,16,8,512]{3,0,2,1:T(8,128)S(1)} %add.1833), channel_id=1, source_target_pairs={{0,8},{2,10},{4,12},{6,14},{8,0},{10,2},{12,4},{14,6},{16,24},{18,... | collective-permute-start | bytes 6291464 | tf_op jit(solution)/shard_map/ppermute | solution.py:145
  443.5 91.9 %collective-permute-start.3 = (f32[8,16,8,512]{3,0,2,1:T(8,128)S(1)}, f32[8,16,8,512]{3,0,2,1:T(8,128)}, u32[]{:S(2)}, u32[]{:S(2)}) collective-permute-start(f32[8,16,8,512]{3,0,2,1:T(8,128)S(1)} %add.1834), channel_id=1, source_target_pairs={{0,16},{2,18},{4,20},{6,22},{8,24},{10,26},{12,28},{14,30},{16,0},... | collective-permute-start | bytes 6291464 | tf_op jit(solution)/shard_map/ppermute | solution.py:145
  763.1 4.4 collective-permute-start.4
  769.5 47.7 %collective-permute-start.5 = (f32[8,16,8,512]{3,0,2,1:T(8,128)S(1)}, f32[8,16,8,512]{3,0,2,1:T(8,128)S(1)}, u32[]{:S(2)}, u32[]{:S(2)}) collective-permute-start(f32[8,16,8,512]{3,0,2,1:T(8,128)S(1)} %add.1933), channel_id=1, source_target_pairs={{0,4},{2,6},{4,0},{6,2},{8,12},{10,14},{12,8},{14,10},{16,20},{18,... | collective-permute-start | bytes 6291464 | tf_op jit(solution)/shard_map/ppermute | solution.py:145
  819.0 47.1 %collective-permute-start.6 = (f32[8,16,8,512]{3,0,2,1:T(8,128)}, f32[8,16,8,512]{3,0,2,1:T(8,128)}, u32[]{:S(2)}, u32[]{:S(2)}) collective-permute-start(f32[8,16,8,512]{3,0,2,1:T(8,128)} %add.1934), channel_id=1, source_target_pairs={{0,8},{2,10},{4,12},{6,14},{8,0},{10,2},{12,4},{14,6},{16,24},{18,... | collective-permute-start | bytes 6291464 | tf_op jit(solution)/shard_map/ppermute | solution.py:145
  870.2 92.1 %collective-permute-start.7 = (f32[8,16,8,512]{3,0,2,1:T(8,128)}, f32[8,16,8,512]{3,0,2,1:T(8,128)}, u32[]{:S(2)}, u32[]{:S(2)}) collective-permute-start(f32[8,16,8,512]{3,0,2,1:T(8,128)} %add.1935), channel_id=1, source_target_pairs={{0,16},{2,18},{4,20},{6,22},{8,24},{10,26},{12,28},{14,30},{16,0},... | collective-permute-start | bytes 6291464 | tf_op jit(solution)/shard_map/ppermute | solution.py:145
  878.0 426.6 %all-reduce.5.cloned.1.call-start = ((), (), s32[]{:S(2)}) async-start(), calls=%async_computation.2 | async-start | bytes 2097152 | tf_op jit(solution)/shard_map/psum | solution.py:154
  1159.1 4.2 collective-permute-start.8
  1163.8 47.7 %collective-permute-start.9 = (f32[8,16,8,512]{3,0,2,1:T(8,128)S(1)}, f32[8,16,8,512]{3,0,2,1:T(8,128)S(1)}, u32[]{:S(2)}, u32[]{:S(2)}) collective-permute-start(f32[8,16,8,512]{3,0,2,1:T(8,128)S(1)} %add.2037), channel_id=1, source_target_pairs={{0,4},{2,6},{4,0},{6,2},{8,12},{10,14},{12,8},{14,10},{16,20},{18,... | collective-permute-start | bytes 6291464 | tf_op jit(solution)/shard_map/ppermute | solution.py:145
  1212.2 46.9 %collective-permute-start.10 = (f32[8,16,8,512]{3,0,2,1:T(8,128)S(1)}, f32[8,16,8,512]{3,0,2,1:T(8,128)S(1)}, u32[]{:S(2)}, u32[]{:S(2)}) collective-permute-start(f32[8,16,8,512]{3,0,2,1:T(8,128)S(1)} %add.2038), channel_id=1, source_target_pairs={{0,8},{2,10},{4,12},{6,14},{8,0},{10,2},{12,4},{14,6},{16,24},{18,... | collective-permute-start | bytes 6291464 | tf_op jit(solution)/shard_map/ppermute | solution.py:145
  1260.8 92.1 %collective-permute-start.11 = (f32[8,16,8,512]{3,0,2,1:T(8,128)}, f32[8,16,8,512]{3,0,2,1:T(8,128)}, u32[]{:S(2)}, u32[]{:S(2)}) collective-permute-start(f32[8,16,8,512]{3,0,2,1:T(8,128)} %add.2039), channel_id=1, source_target_pairs={{0,16},{2,18},{4,20},{6,22},{8,24},{10,26},{12,28},{14,30},{16,0},... | collective-permute-start | bytes 6291464 | tf_op jit(solution)/shard_map/ppermute | solution.py:145
  (114 other events, 957.7 us)
Sparse Core Ops, SparseCore 0:
  10.3 129.1 all-gather.1
  878.2 40.0 all-reduce.2
  1264.4 40.1 all-reduce.4
